TPU v7x, 32 devices: a whole 2x2x4 slice. The times are simulated.
32 devices in a mesh: lon: 8 (over y, x, core), mem: 4 (over z).
Axes of the slice: x: 2, y: 2, z: 4, core: 2. Of those that a mesh axis runs over, the one named last changes fastest.
Arguments:
- sample_collection: bfloat16 [256, 3, 1, 16, 1024], P('mem', None, None, None, 'lon'), may hold values from -6 to 6
- layer_depth: float32 [1, 16, 1024], P(None, None, 'lon'), may hold values from 0.05 to 0.2
- obs_where: int32 [4, 8, 512], P('mem', 'lon'), may hold values from 0 to 4895, as said below
- observed_values: float32 [4, 8, 512], P('mem', 'lon'), may hold values from -6 to 6
- obs_precision: float32 [4, 8, 512], P('mem', 'lon'), may hold values from 0.5 to 4
- loc_index: int32 [4, 8, 512], P('mem', 'lon'), may hold values from 0 to 15
- obs_count: int32 [4, 8], P('mem', 'lon'), may hold values from 64 to 512, as said below
Outputs:
- analysis: bfloat16 [256, 3, 1, 16, 1024], P('mem', None, None, None, 'lon')
Inputs may be any that keep to these rules, and one draw needn't show every extreme that they name: `obs_where`: flat index into a block's region of 3 x 1 x (12) x (136) cells (component, layer, row, column). Slots o < obs_count of a block hold observations; in each draw some block has all 512.
All inputs are finite; a program needn't handle non-finite values.
Results may differ from a plain program's by a relative error of at most 0.0037.
The roundings to bfloat16 on the way count: a program that leaves them out, or rounds other values in their place, can miss the bound.
Values may be sent and summed in bfloat16 or wider, within the bound.
A program may use at most 128 MiB of HBM per device.

v0:
```python
import math

import jax
import jax.numpy as jnp
from jax import lax
from jax.sharding import PartitionSpec as P

STEPS = 2
MARGIN_WIDTH = 4
BAND = 4
CLON = 128
NS_ITERS = 5


time_step = 0.8
inflation = 1.1


def extended(value, sides, width, wrap):
    for axis, dim in sides:
        count, length = (lax.axis_size(axis), value.shape[dim])
        up = [(i, (i + 1) % count) for i in range(count if wrap else count - 1)]
        down = [(j, i) for i, j in up]
        last = lax.slice_in_dim(value, length - width, length, axis=dim)
        initial = lax.slice_in_dim(value, 0, width, axis=dim)
        before = lax.ppermute(last, axis, up)
        after = lax.ppermute(initial, axis, down)
        value = jnp.concatenate([before, value, after], axis=dim)
    return value


def coriolis_rate(count_rows):
    latitude = jnp.arange(count_rows, dtype=jnp.float32)
    return 0.4 * (latitude / (count_rows - 1) - 0.5)


def lat_diff(field):
    bordered_array = jnp.pad(field, [(0, 0)] * (field.ndim - 2) + [(1, 1), (0, 0)])
    return 0.5 * (bordered_array[..., 2:, :] - bordered_array[..., :-2, :])


def lon_diff(field):
    return 0.5 * (field[..., 2:] - field[..., :-2])


def advance(fields, depth_cut, spin_frequency):
    height = fields[..., 0, :, :, :]
    east_wind = fields[..., 1, :, :, :]
    north_wind = fields[..., 2, :, :, :]
    flux_east = depth_cut * east_wind
    flux_north = depth_cut * north_wind
    height_new = height[..., 1:-1] - time_step * (
        lon_diff(flux_east) + lat_diff(flux_north)[..., 1:-1]
    )
    east_new = (
        east_wind[..., 2:-2]
        - time_step * lon_diff(height_new)
        + time_step * spin_frequency * north_wind[..., 2:-2]
    )
    north_new = (
        north_wind[..., 2:-2]
        - time_step * lat_diff(height_new)[..., 1:-1]
        - time_step * spin_frequency * east_wind[..., 2:-2]
    )
    return jnp.stack([height_new[..., 1:-1], east_new, north_new], axis=-4)


def analyse(picked_raw, core_cells, values, precision_vals, locs, count):
    members = core_cells.shape[0]
    highest = lax.Precision.HIGHEST
    picked = picked_raw.astype(jnp.float32)
    slot_total = picked.shape[1]
    slot_index = jnp.arange(slot_total, dtype=jnp.int32)
    live_slots = (slot_index < count).astype(jnp.float32)
    taper_table = (1.0 - jnp.arange(16, dtype=jnp.float32) / 16.0) ** 2
    taper_weight = jnp.sum(
        jnp.where(
            locs[:, None] == jnp.arange(16, dtype=jnp.int32)[None, :], taper_table[None, :], 0.0
        ),
        axis=1,
    )
    weight = precision_vals * taper_weight * live_slots
    obs_mean = jnp.mean(picked, axis=0)
    spread = picked - obs_mean[None, :]
    innovation = values - obs_mean
    weighted = spread * weight[None, :]
    gram_matrix = jnp.dot(weighted, spread.T, precision=highest)
    drive_vector = jnp.dot(weighted, innovation, precision=highest)
    prior = (members - 1) / inflation
    trace_bound = prior + jnp.trace(gram_matrix)
    identity = jnp.eye(members, dtype=jnp.float32)
    root_iter = (gram_matrix + prior * identity) / trace_bound
    inv_root = identity
    for sweep in range(NS_ITERS):
        correction = 1.5 * identity - 0.5 * jnp.dot(inv_root, root_iter, precision=highest)
        root_iter = jnp.dot(root_iter, correction, precision=highest)
        inv_root = jnp.dot(correction, inv_root, precision=highest)
    shrink = inv_root / jnp.sqrt(trace_bound)
    mean_weight = jnp.dot(
        shrink, jnp.dot(shrink, drive_vector, precision=highest), precision=highest
    )
    weights = math.sqrt(members - 1) * shrink + mean_weight[:, None]
    owned_cells = core_cells.reshape(members, -1).astype(jnp.float32)
    cell_mean = jnp.mean(owned_cells, axis=0)
    perturb = owned_cells - cell_mean[None, :]
    analysed = cell_mean[None, :] + jnp.dot(weights.T, perturb, precision=highest)
    return analysed.astype(jnp.bfloat16).reshape(core_cells.shape)


def on_device(
    sample_collection, layer_depth, obs_where, observed_values, obs_precision, loc_index, obs_count
):
    count_rows = sample_collection.shape[3]
    spin_frequency = coriolis_rate(count_rows)[:, None]
    reach = 2 * STEPS
    bordered_thickness_grid = extended(layer_depth, (("lon", 2),), reach, True)
    total = bordered_thickness_grid.shape[-1]
    enlarged_grid = sample_collection.astype(jnp.float32)
    depth_step = bordered_thickness_grid[..., reach - 2 : total - (reach - 2)]
    for step_index in range(STEPS):
        widened = extended(enlarged_grid, (("lon", 4),), 2, True)
        enlarged_grid = advance(widened, depth_step, spin_frequency)
    predicted_solution = enlarged_grid.astype(jnp.bfloat16)
    own_where = obs_where[0, 0]
    latitude_slab = lax.all_to_all(
        predicted_solution, "mem", split_axis=3, concat_axis=0, tiled=True
    )
    tall_band = extended(latitude_slab, (("mem", 3),), MARGIN_WIDTH, False)
    region = extended(tall_band, (("lon", 4),), MARGIN_WIDTH, True)
    picked_raw = jnp.take(region.reshape(region.shape[0], -1), own_where, axis=1)
    core_cells = region[
        :, :, :, MARGIN_WIDTH : MARGIN_WIDTH + BAND, MARGIN_WIDTH : MARGIN_WIDTH + CLON
    ]
    analysed = analyse(
        picked_raw,
        core_cells,
        observed_values[0, 0],
        obs_precision[0, 0],
        loc_index[0, 0],
        obs_count[0, 0],
    )
    return lax.all_to_all(analysed, "mem", split_axis=0, concat_axis=3, tiled=True)


def solution(mesh):
    in_specs = (
        P("mem", None, None, None, "lon"),
        P(None, None, "lon"),
        P("mem", "lon", None),
        P("mem", "lon", None),
        P("mem", "lon", None),
        P("mem", "lon", None),
        P("mem", "lon"),
    )
    out_specs = P("mem", None, None, None, "lon")
    return jax.shard_map(
        on_device, mesh=mesh, in_specs=in_specs, out_specs=out_specs, check_vma=False
    )
```

profile of v0, /device:TPU:0, one launch (start us, length us, event | category | flops | bytes accessed | tf_op | source)
XLA Modules:
  0.0 120.4 jit_solution(7594350822294012409)
XLA Ops:
  0.0 0.8 fusion.61
  1.3 2.9 %collective-permute-start.3 = (f32[1,16,4]{2,1,0:T(8,128)S(1)}, f32[1,16,4]{2,1,0:T(8,128)S(1)}, u32[]{:S(2)}, u32[]{:S(2)}) collective-permute-start(f32[1,16,4]{2,1,0:T(8,128)S(1)} %get-tuple-element.37), channel_id=1, source_target_pairs={{4,0},{8,4},{12,8},{16,12},{20,16},{24,20},{28,24},{0,28},{5,1},{9... | collective-permute-start | bytes 776 | tf_op jit(solution)/shard_map/ppermute | solution.py:27
  4.2 2.3 %copy.31 = bf16[64,3,1,16,128]{0,3,4,2,1:T(8,128)(2,1)S(1)} copy(bf16[64,3,1,16,128]{4,3,2,1,0:T(8,128)(2,1)} %param.7) | data formatting | bytes 1572864 | tf_op args[0]
  6.7 2.6 %collective-permute-start.1 = (f32[64,3,1,16,2]{0,3,4,2,1:T(8,128)S(1)}, f32[64,3,1,16,2]{0,3,4,2,1:T(8,128)S(1)}, u32[]{:S(2)}, u32[]{:S(2)}) collective-permute-start(f32[64,3,1,16,2]{0,3,4,2,1:T(8,128)S(1)} %get-tuple-element.24), channel_id=1, source_target_pairs={{4,0},{8,4},{12,8},{16,12},{20,16},{24,20},{28,24},{0,28},{5,1},{9... | collective-permute-start | bytes 73736 | tf_op jit(solution)/shard_map/ppermute | solution.py:27
  9.3 1.7 %convert_element_type.35 = f32[64,3,1,16,128]{0,3,4,2,1:T(8,128)S(1)} convert(bf16[64,3,1,16,128]{0,3,4,2,1:T(8,128)(2,1)} %copy-done) | non-fusion elementwise | flops 393216 | bytes 2359296 | tf_op jit(solution)/shard_map/convert_element_type | solution.py:118
  13.5 0.9 collective-permute-start.4
  14.4 1.8 %collective-permute-start.5 = (f32[64,3,1,16,2]{0,3,4,2,1:T(8,128)S(1)}, f32[64,3,1,16,2]{0,3,4,2,1:T(8,128)S(1)}, u32[]{:S(2)}, u32[]{:S(2)}) collective-permute-start(f32[64,3,1,16,2]{0,3,4,2,1:T(8,128)S(1)} %get-tuple-element.16), channel_id=1, source_target_pairs={{4,0},{8,4},{12,8},{16,12},{20,16},{24,20},{28,24},{0,28},{5,1},{9... | collective-permute-start | bytes 73736 | tf_op jit(solution)/shard_map/ppermute | solution.py:27
  16.2 1.8 %collective-permute-done.4 = f32[64,3,1,16,2]{0,3,4,2,1:T(8,128)S(1)} collective-permute-done((f32[64,3,1,16,2]{0,3,4,2,1:T(8,128)S(1)}, f32[64,3,1,16,2]{0,3,4,2,1:T(8,128)S(1)}, u32[]{:S(2)}, u32[]{:S(2)}) %collective-permute-start.4) | collective-permute-done | bytes 24608 | tf_op jit(solution)/shard_map/ppermute | solution.py:26
  20.7 1.2 copy.33
  21.9 26.4 %all_to_all.36 = bf16[64,3,1,16,128]{4,0,2,1,3:T(8,128)(2,1)S(1)} all-to-all(bf16[64,3,1,16,128]{4,0,2,1,3:T(8,128)(2,1)S(1)} %copy.33), channel_id=1, replica_groups=mesh['lon'=8,'mem'=4] {'mem'}, dimensions={3} | all-to-all | bytes 1572864 | tf_op jit(solution)/shard_map/all_to_all | solution.py:125
  48.3 1.7 %fusion.60 = (bf16[64,3,1,4,4,128]{5,4,1,0,3,2:T(4,128)(2,1)}, f32[4,64,3,1,4,128]{5,4,2,1,0,3:T(4,128)S(1)}) fusion(bf16[64,3,1,4,4,128]{5,0,1,4,3,2:T(8,128)(2,1)S(1)} %bitcast.101), kind=kLoop, calls=%fused_computation.130 | loop fusion | flops 393216 | bytes 3145728 | tf_op jit(solution)/shard_map/all_to_all | solution.py:125
  50.0 1.6 %copy.35 = bf16[256,3,1,4,128]{0,4,3,1,2:T(8,128)(2,1)S(1)} copy(bf16[256,3,1,4,128]{4,3,1,0,2:T(4,128)(2,1)} %bitcast.105) | data formatting | bytes 1572864 | tf_op jit(solution)/shard_map/all_to_all | solution.py:125
  51.6 1.3 %collective-permute-start.7 = (bf16[256,3,1,4,128]{0,4,3,1,2:T(8,128)(2,1)S(1)}, bf16[256,3,1,4,128]{0,4,3,1,2:T(8,128)(2,1)S(1)}, u32[]{:S(2)}, u32[]{:S(2)}) collective-permute-start(bf16[256,3,1,4,128]{0,4,3,1,2:T(8,128)(2,1)S(1)} %copy.35), channel_id=1, source_target_pairs={{1,0},{2,1},{3,2},{5,4},{6,5},{7,6},{9,8},{10,9},{11,10},{13,12},{... | collective-permute-start | bytes 2359304 | tf_op jit(solution)/shard_map/ppermute | solution.py:27
  52.9 4.6 %collective-permute-start.6 = (bf16[256,3,1,4,128]{0,4,3,1,2:T(8,128)(2,1)S(1)}, bf16[256,3,1,4,128]{0,4,3,1,2:T(8,128)(2,1)S(1)}, u32[]{:S(2)}, u32[]{:S(2)}) collective-permute-start(bf16[256,3,1,4,128]{0,4,3,1,2:T(8,128)(2,1)S(1)} %copy.35), channel_id=1, source_target_pairs={{0,1},{1,2},{2,3},{4,5},{5,6},{6,7},{8,9},{9,10},{10,11},{12,13},{... | collective-permute-start | bytes 2359304 | tf_op jit(solution)/shard_map/ppermute | solution.py:26
  58.8 13.3 %collective-permute-done.7 = bf16[256,3,1,4,128]{0,4,3,1,2:T(8,128)(2,1)S(1)} collective-permute-done((bf16[256,3,1,4,128]{0,4,3,1,2:T(8,128)(2,1)S(1)}, bf16[256,3,1,4,128]{0,4,3,1,2:T(8,128)(2,1)S(1)}, u32[]{:S(2)}, u32[]{:S(2)}) %collective-permute-start.7) | collective-permute-done | bytes 786464 | tf_op jit(solution)/shard_map/ppermute | solution.py:27
  72.2 1.2 collective-permute-done.6
  74.2 2.6 %collective-permute-start.9 = (bf16[256,3,1,12,4]{0,4,3,1,2:T(4,128)(2,1)S(1)}, bf16[256,3,1,12,4]{0,4,3,1,2:T(4,128)(2,1)S(1)}, u32[]{:S(2)}, u32[]{:S(2)}) collective-permute-start(bf16[256,3,1,12,4]{0,4,3,1,2:T(4,128)(2,1)S(1)} %get-tuple-element.18), channel_id=1, source_target_pairs={{4,0},{8,4},{12,8},{16,12},{20,16},{24,20},{28,24},{0,28},{5,1},{9... | collective-permute-start | bytes 221192 | tf_op jit(solution)/shard_map/ppermute | solution.py:27
  76.9 1.8 %reshape.196 = f32[256,1536]{1,0:T(8,128)} reshape(f32[4,64,3,1,4,128]{5,4,2,1,0,3:T(4,128)S(1)} %get-tuple-element.35) | data formatting | bytes 3145728 | tf_op jit(solution)/shard_map/convert_element_type | solution.py:103
  79.0 2.5 %pad_maximum_fusion.2 = bf16[256,3,1,12,136]{0,4,3,1,2:T(8,128)(2,1)S(1)} fusion(bf16[256,3,1,12,4]{0,4,3,1,2:T(4,128)(2,1)S(1)} %collective-permute-done.9, bf16[256,3,1,4,128]{0,4,3,1,2:T(8,128)(2,1)} %copy-done.2, bf16[256,3,1,4,128]{0,4,3,1,2:T(8,128)(2,1)S(1)} %copy.35, bf16[256,3,1,4,128]{0,4,3,1,2:T(8,128)(2,1)} %copy-done.3, ...), kind=kLoop, calls=%fused_computation.5 | loop fusion | flops 12533760 | bytes 5013504 | tf_op jit(solution)/shard_map/concatenate | solution.py:28
  81.6 2.0 %gather_fusion = bf16[512,256]{1,0:T(8,128)(2,1)S(1)} fusion(bf16[256,4896]{0,1:T(8,128)(2,1)S(1)} %bitcast.100, s32[1024]{0:T(1024)S(1)} %pad_clamp_fusion), kind=kCustom, calls=%fused_computation | custom fusion | bytes 526336 | tf_op jit(solution)/shard_map/jit(_take)/gather | solution.py:130
  83.8 2.0 %select_reduce_fusion = (f32[]{:T(128)}, f32[256,256]{1,0:T(8,128)S(1)}) fusion(f32[512]{0:T(512)S(1)} %get-tuple-element.39, bf16[512,256]{1,0:T(8,128)(2,1)S(1)} %gather_fusion, pred[512]{0:T(512)(128)(4,1)S(1)} %compare_and_fusion, f32[512]{0:T(512)S(1)} %get-tuple-element.42), kind=kOutput, calls=%fused_computation.94 | convolution fusion | flops 403767296 | bytes 528900 | tf_op jit(solution)/shard_map/dot_general | solution.py:87
  92.9 1.6 %fusion = bf16[256,1536]{1,0:T(8,128)(2,1)S(1)} fusion(f32[256,1536]{1,0:T(8,128)S(1)} %copy-done.1, f32[1536]{0:T(1024)S(1)} %div.41, f32[256,256]{1,0:T(8,128)S(1)} %convolution_divide_fusion, f32[256]{0:T(256)S(1)} %bitcast.108), kind=kOutput, calls=%fused_computation.4 | convolution fusion | flops 1209270272 | bytes 2628608 | tf_op jit(solution)/shard_map/dot_general | solution.py:106
  94.7 24.5 %all_to_all.37 = bf16[256,3,1,4,128]{4,3,1,2,0:T(4,128)(2,1)S(1)} all-to-all(bf16[256,3,1,4,128]{4,3,1,2,0:T(4,128)(2,1)S(1)} %bitcast.103), channel_id=1, replica_groups=mesh['lon'=8,'mem'=4] {'mem'}, dimensions={0} | all-to-all | bytes 1572864 | tf_op jit(solution)/shard_map/all_to_all | solution.py:142
  119.2 1.2 copy.39
  (78 shorter events, 14.4 us)
Async XLA Ops:
  0.8 10.2 %collective-permute-start.2 = (f32[1,16,4]{2,1,0:T(8,128)S(1)}, f32[1,16,4]{2,1,0:T(8,128)S(1)}, u32[]{:S(2)}, u32[]{:S(2)}) collective-permute-start(f32[1,16,4]{2,1,0:T(8,128)S(1)} %get-tuple-element.36), channel_id=1, source_target_pairs={{0,4},{4,8},{8,12},{12,16},{16,20},{20,24},{24,28},{28,0},{1,5},{5... | collective-permute-start | bytes 776 | tf_op jit(solution)/shard_map/ppermute | solution.py:26
  1.3 9.7 %collective-permute-start.3 = (f32[1,16,4]{2,1,0:T(8,128)S(1)}, f32[1,16,4]{2,1,0:T(8,128)S(1)}, u32[]{:S(2)}, u32[]{:S(2)}) collective-permute-start(f32[1,16,4]{2,1,0:T(8,128)S(1)} %get-tuple-element.37), channel_id=1, source_target_pairs={{4,0},{8,4},{12,8},{16,12},{20,16},{24,20},{28,24},{0,28},{5,1},{9... | collective-permute-start | bytes 776 | tf_op jit(solution)/shard_map/ppermute | solution.py:27
  6.6 2.7 %copy-start = (bf16[64,3,1,16,128]{0,3,4,2,1:T(8,128)(2,1)}, bf16[64,3,1,16,128]{0,3,4,2,1:T(8,128)(2,1)S(1)}, u32[]{:S(2)}) copy-start(bf16[64,3,1,16,128]{0,3,4,2,1:T(8,128)(2,1)S(1)} %copy.31) | copy-start | bytes 2359300
  6.6 4.6 %collective-permute-start = (f32[64,3,1,16,2]{0,3,4,2,1:T(8,128)S(1)}, f32[64,3,1,16,2]{0,3,4,2,1:T(8,128)S(1)}, u32[]{:S(2)}, u32[]{:S(2)}) collective-permute-start(f32[64,3,1,16,2]{0,3,4,2,1:T(8,128)S(1)} %get-tuple-element.23), channel_id=1, source_target_pairs={{0,4},{4,8},{8,12},{12,16},{16,20},{20,24},{24,28},{28,0},{1,5},{5... | collective-permute-start | bytes 73736 | tf_op jit(solution)/shard_map/ppermute | solution.py:26
  6.7 4.6 %collective-permute-start.1 = (f32[64,3,1,16,2]{0,3,4,2,1:T(8,128)S(1)}, f32[64,3,1,16,2]{0,3,4,2,1:T(8,128)S(1)}, u32[]{:S(2)}, u32[]{:S(2)}) collective-permute-start(f32[64,3,1,16,2]{0,3,4,2,1:T(8,128)S(1)} %get-tuple-element.24), channel_id=1, source_target_pairs={{4,0},{8,4},{12,8},{16,12},{20,16},{24,20},{28,24},{0,28},{5,1},{9... | collective-permute-start | bytes 73736 | tf_op jit(solution)/shard_map/ppermute | solution.py:27
  9.3 1.7 %copy-start.4 = (f32[1,16,128]{2,1,0:T(8,128)S(1)}, f32[1,16,128]{2,1,0:T(8,128)}, u32[]{:S(2)}) copy-start(f32[1,16,128]{2,1,0:T(8,128)} %param.8) | copy-start | bytes 24580
  13.5 4.5 %collective-permute-start.4 = (f32[64,3,1,16,2]{0,3,4,2,1:T(8,128)S(1)}, f32[64,3,1,16,2]{0,3,4,2,1:T(8,128)S(1)}, u32[]{:S(2)}, u32[]{:S(2)}) collective-permute-start(f32[64,3,1,16,2]{0,3,4,2,1:T(8,128)S(1)} %get-tuple-element.15), channel_id=1, source_target_pairs={{0,4},{4,8},{8,12},{12,16},{16,20},{20,24},{24,28},{28,0},{1,5},{5... | collective-permute-start | bytes 73736 | tf_op jit(solution)/shard_map/ppermute | solution.py:26
  14.4 3.6 %collective-permute-start.5 = (f32[64,3,1,16,2]{0,3,4,2,1:T(8,128)S(1)}, f32[64,3,1,16,2]{0,3,4,2,1:T(8,128)S(1)}, u32[]{:S(2)}, u32[]{:S(2)}) collective-permute-start(f32[64,3,1,16,2]{0,3,4,2,1:T(8,128)S(1)} %get-tuple-element.16), channel_id=1, source_target_pairs={{4,0},{8,4},{12,8},{16,12},{20,16},{24,20},{28,24},{0,28},{5,1},{9... | collective-permute-start | bytes 73736 | tf_op jit(solution)/shard_map/ppermute | solution.py:27
  50.0 7.5 %copy-start.5 = (s32[1,1,512]{2,1,0:T(1,128)S(1)}, s32[1,1,512]{2,1,0:T(1,128)}, u32[]{:S(2)}) copy-start(s32[1,1,512]{2,1,0:T(1,128)} %param.9) | copy-start | bytes 6148
  50.0 8.2 %copy-start.6 = (s32[1,1,512]{2,1,0:T(1,128)S(1)}, s32[1,1,512]{2,1,0:T(1,128)}, u32[]{:S(2)}) copy-start(s32[1,1,512]{2,1,0:T(1,128)} %param.12) | copy-start | bytes 6148
  51.6 20.6 %collective-permute-start.7 = (bf16[256,3,1,4,128]{0,4,3,1,2:T(8,128)(2,1)S(1)}, bf16[256,3,1,4,128]{0,4,3,1,2:T(8,128)(2,1)S(1)}, u32[]{:S(2)}, u32[]{:S(2)}) collective-permute-start(bf16[256,3,1,4,128]{0,4,3,1,2:T(8,128)(2,1)S(1)} %copy.35), channel_id=1, source_target_pairs={{1,0},{2,1},{3,2},{5,4},{6,5},{7,6},{9,8},{10,9},{11,10},{13,12},{... | collective-permute-start | bytes 2359304 | tf_op jit(solution)/shard_map/ppermute | solution.py:27
  52.9 20.5 %collective-permute-start.6 = (bf16[256,3,1,4,128]{0,4,3,1,2:T(8,128)(2,1)S(1)}, bf16[256,3,1,4,128]{0,4,3,1,2:T(8,128)(2,1)S(1)}, u32[]{:S(2)}, u32[]{:S(2)}) collective-permute-start(bf16[256,3,1,4,128]{0,4,3,1,2:T(8,128)(2,1)S(1)} %copy.35), channel_id=1, source_target_pairs={{0,1},{1,2},{2,3},{4,5},{5,6},{6,7},{8,9},{9,10},{10,11},{12,13},{... | collective-permute-start | bytes 2359304 | tf_op jit(solution)/shard_map/ppermute | solution.py:26
  72.2 1.2 copy-start.2
  73.3 0.9 copy-start.3
  74.2 4.7 %collective-permute-start.8 = (bf16[256,3,1,12,4]{0,4,3,1,2:T(4,128)(2,1)S(1)}, bf16[256,3,1,12,4]{0,4,3,1,2:T(4,128)(2,1)S(1)}, u32[]{:S(2)}, u32[]{:S(2)}) collective-permute-start(bf16[256,3,1,12,4]{0,4,3,1,2:T(4,128)(2,1)S(1)} %get-tuple-element.17), channel_id=1, source_target_pairs={{0,4},{4,8},{8,12},{12,16},{16,20},{20,24},{24,28},{28,0},{1,5},{5... | collective-permute-start | bytes 221192 | tf_op jit(solution)/shard_map/ppermute | solution.py:26
  74.2 4.7 %collective-permute-start.9 = (bf16[256,3,1,12,4]{0,4,3,1,2:T(4,128)(2,1)S(1)}, bf16[256,3,1,12,4]{0,4,3,1,2:T(4,128)(2,1)S(1)}, u32[]{:S(2)}, u32[]{:S(2)}) collective-permute-start(bf16[256,3,1,12,4]{0,4,3,1,2:T(4,128)(2,1)S(1)} %get-tuple-element.18), channel_id=1, source_target_pairs={{4,0},{8,4},{12,8},{16,12},{20,16},{24,20},{28,24},{0,28},{5,1},{9... | collective-permute-start | bytes 221192 | tf_op jit(solution)/shard_map/ppermute | solution.py:27
  81.5 2.2 %copy-start.7 = (f32[1,1,512]{2,1,0:T(1,128)S(1)}, f32[1,1,512]{2,1,0:T(1,128)}, u32[]{:S(2)}) copy-start(f32[1,1,512]{2,1,0:T(1,128)} %param.10) | copy-start | bytes 6148
  81.6 2.2 %copy-start.8 = (f32[1,1,512]{2,1,0:T(1,128)S(1)}, f32[1,1,512]{2,1,0:T(1,128)}, u32[]{:S(2)}) copy-start(f32[1,1,512]{2,1,0:T(1,128)} %param.11) | copy-start | bytes 6148
  91.5 1.5 %copy-start.1 = (f32[256,1536]{1,0:T(8,128)S(1)}, f32[256,1536]{1,0:T(8,128)}, u32[]{:S(2)}) copy-start(f32[256,1536]{1,0:T(8,128)} %reshape.196) | copy-start | bytes 4718596
where the time goes:
time: 121 us; the launch traced here: 120 us
  blocking collectives  50.9 us (42%)
  starting transfers between devices  17.3 us (14%)
  waiting for transfers between devices  16.6 us (14%)
  local copies, waits for them, and re-layouts  13.5 us (11%)
  other arithmetic  10.4 us (9%)
  matrix products  9.9 us (8%)
  between operations  1.81 us (1%)
    all_to_all x1, blocking collectives, on_device(): lax.all_to_all(predicted_solution, 'mem', split_axis=3, concat_axis=0, ti...  26.4 us
    all_to_all x1, blocking collectives, on_device(): lax.all_to_all(analysed, 'mem', split_axis=0, concat_axis=3, tiled=True)  24.5 us
    ppermute x5, waiting for transfers between devices, extended(): after = lax.ppermute(initial, axis, down)  13.3 us
    ppermute x5, starting transfers between devices, extended(): after = lax.ppermute(initial, axis, down)  11.2 us
    ppermute x5, starting transfers between devices, extended(): before = lax.ppermute(last, axis, up)  6.05 us
    ppermute x5, waiting for transfers between devices, extended(): before = lax.ppermute(last, axis, up)  3.25 us
    unnamed x19, local copies, waits for them, and re-layouts  3.23 us
    concatenate x3, other arithmetic, extended(): value = jnp.concatenate([before, value, after], axis=dim)  3.13 us
  transfers between devices with their start and end apart: 10, of which 4 were waited for; matrix products, arithmetic and copies ran while one was open for 6% of the time, Pallas kernels for 0%

commit v1 on v0

v1 whole, which is shorter than its diff:
```python
import functools
import math

import jax
import jax.numpy as jnp
from jax import lax
from jax.experimental import pallas as pl
from jax.experimental.pallas import tpu as pltpu
from jax.sharding import PartitionSpec as P

STEPS = 2
MARGIN_WIDTH = 4
BAND = 4
NS_ITERS = 5
MESH = pl.DeviceIdType.MESH
HIGHEST = lax.Precision.HIGHEST

time_step = 0.8
inflation = 1.1


def coriolis_rate(count_rows):
    latitude = jnp.arange(count_rows, dtype=jnp.float32)
    return 0.4 * (latitude / (count_rows - 1) - 0.5)


def lat_diff(field):
    bordered_array = jnp.pad(field, [(0, 0)] * (field.ndim - 2) + [(1, 1), (0, 0)])
    return 0.5 * (bordered_array[..., 2:, :] - bordered_array[..., :-2, :])


def lon_diff(field):
    return 0.5 * (field[..., 2:] - field[..., :-2])


def advance(fields, depth_cut, spin_frequency):
    height = fields[..., 0, :, :, :]
    east_wind = fields[..., 1, :, :, :]
    north_wind = fields[..., 2, :, :, :]
    flux_east = depth_cut * east_wind
    flux_north = depth_cut * north_wind
    height_new = height[..., 1:-1] - time_step * (
        lon_diff(flux_east) + lat_diff(flux_north)[..., 1:-1]
    )
    east_new = (
        east_wind[..., 2:-2]
        - time_step * lon_diff(height_new)
        + time_step * spin_frequency * north_wind[..., 2:-2]
    )
    north_new = (
        north_wind[..., 2:-2]
        - time_step * lat_diff(height_new)[..., 1:-1]
        - time_step * spin_frequency * east_wind[..., 2:-2]
    )
    return jnp.stack([height_new[..., 1:-1], east_new, north_new], axis=-4)


def extended_lon(value, width):
    count, length = lax.axis_size("lon"), value.shape[-1]
    up = [(i, (i + 1) % count) for i in range(count)]
    down = [(j, i) for i, j in up]
    before = lax.ppermute(value[..., length - width :], "lon", up)
    after = lax.ppermute(value[..., :width], "lon", down)
    return jnp.concatenate([before, value, after], axis=-1)


def exchange_order(n):
    return sorted(range(1, n), key=lambda d: (-min(d, n - d), d))


def analysis_kernel(
    n, picks_ref, cells_ref, values_ref, weight_ref, out_ref,
    picked, cells, result, transform, pick_send, pick_recv, cell_send, cell_recv, back_send, back_recv,
):
    me = lax.axis_index("mem")
    group = cells_ref.shape[1]
    members = n * group

    barrier = pltpu.get_barrier_semaphore()
    for d in range(1, n):
        pl.semaphore_signal(
            barrier, inc=1, device_id={"mem": lax.rem(me + d, n)}, device_id_type=MESH
        )
    pl.semaphore_wait(barrier, n - 1)

    def send(src, dst, ss, rs, d):
        peer = lax.rem(me + d, n)
        return pltpu.make_async_remote_copy(
            src_ref=src, dst_ref=dst, send_sem=ss.at[d], recv_sem=rs.at[d],
            device_id={"mem": peer}, device_id_type=MESH,
        )

    order = exchange_order(n)
    pick_copies = [
        send(picks_ref.at[d], picked.at[me], pick_send, pick_recv, d) for d in order
    ]
    for copy in pick_copies:
        copy.start()
    cell_copies = [
        send(cells_ref.at[lax.rem(me + d, n)], cells.at[me], cell_send, cell_recv, d)
        for d in order
    ]
    for copy in cell_copies:
        copy.start()
    picked[me] = picks_ref[0]
    cells[me] = cells_ref[me]
    for copy in pick_copies:
        copy.wait()

    obs = picked[...].astype(jnp.float32).reshape(members, -1)
    obs_mean = jnp.mean(obs, axis=0, keepdims=True)
    spread = obs - obs_mean
    weighted = spread * weight_ref[...]
    innovation = values_ref[...] - obs_mean

    def mm(a, b):
        return jnp.dot(a, b, precision=HIGHEST, preferred_element_type=jnp.float32)

    gram = lax.dot_general(
        weighted, spread, (((1,), (1,)), ((), ())),
        precision=HIGHEST, preferred_element_type=jnp.float32,
    )
    drive = jnp.sum(weighted * innovation, axis=1, keepdims=True)
    prior = (members - 1) / inflation
    trace = jnp.sum(jnp.sum(weighted * spread, axis=1, keepdims=True), axis=0, keepdims=True)
    trace_bound = prior + trace
    row_at = lax.broadcasted_iota(jnp.int32, (members, members), 0)
    column_at = lax.broadcasted_iota(jnp.int32, (members, members), 1)
    identity = jnp.where(row_at == column_at, 1.0, 0.0).astype(jnp.float32)
    root_iter = (gram + prior * identity) / trace_bound
    correction = 1.5 * identity - 0.5 * root_iter
    root_iter = mm(root_iter, correction)
    inv_root = correction
    for sweep in range(1, NS_ITERS):
        correction = 1.5 * identity - 0.5 * mm(inv_root, root_iter)
        if sweep < NS_ITERS - 1:
            root_iter = mm(root_iter, correction)
        inv_root = mm(correction, inv_root)
    shrink = inv_root * lax.rsqrt(trace_bound)
    inner = jnp.sum(shrink * drive, axis=0, keepdims=True)
    mean_weight = jnp.sum(shrink * inner, axis=1, keepdims=True)
    weights = math.sqrt(members - 1) * shrink + mean_weight
    weights = weights + (1.0 - jnp.sum(weights, axis=0, keepdims=True)) / members
    weights_t = weights.T
    high = weights_t.astype(jnp.bfloat16)
    transform[0] = high
    transform[1] = (weights_t - high.astype(jnp.float32)).astype(jnp.bfloat16)

    for copy in cell_copies:
        copy.wait()
    all_cells = cells[...].reshape(members, -1)

    def analysed(peer):
        rows = pl.ds(pl.multiple_of(peer * group, group), group)
        total = jnp.dot(transform[0, rows, :], all_cells, preferred_element_type=jnp.float32)
        total += jnp.dot(transform[1, rows, :], all_cells, preferred_element_type=jnp.float32)
        return total.astype(jnp.bfloat16)

    back_copies = []
    for d in order:
        peer = lax.rem(me + d, n)
        result[d] = analysed(peer)
        copy = send(result.at[d], out_ref.at[me], back_send, back_recv, d)
        copy.start()
        back_copies.append(copy)
    out_ref[me] = analysed(me)
    for copy in back_copies:
        copy.wait()


def on_device(
    sample_collection, layer_depth, obs_where, observed_values, obs_precision, loc_index, obs_count
):
    n = lax.axis_size("mem")
    me = lax.axis_index("mem")
    group, _, _, count_rows, strip = sample_collection.shape
    slots = obs_where.shape[-1]
    wheres = [obs_where[0, 0]]
    for d in range(1, n):
        pairs = [((i + d) % n, i) for i in range(n)]
        wheres.append(lax.ppermute(obs_where[0, 0], "mem", pairs))

    spin_frequency = coriolis_rate(count_rows)[:, None]
    reach = 2 * STEPS + MARGIN_WIDTH
    depth = extended_lon(layer_depth, reach)
    fields = extended_lon(sample_collection, reach).astype(jnp.float32)
    for step_index in range(STEPS):
        fields = advance(
            fields, depth[..., 2 * step_index : depth.shape[-1] - 2 * step_index], spin_frequency
        )
    fore = fields.astype(jnp.bfloat16)[:, :, 0]
    own = fore[..., MARGIN_WIDTH : MARGIN_WIDTH + strip]
    cells = own.reshape(group, 3, n, BAND, strip).transpose(2, 0, 1, 3, 4).reshape(n, group, -1)

    padded = jnp.pad(fore, ((0, 0), (0, 0), (MARGIN_WIDTH, MARGIN_WIDTH), (0, 0)))
    tall, wide = count_rows + 2 * MARGIN_WIDTH, strip + 2 * MARGIN_WIDTH
    area = (BAND + 2 * MARGIN_WIDTH) * wide
    flat = padded.reshape(group, -1)
    picks = []
    for d in range(n):
        band = lax.rem(me + d, n)
        component = wheres[d] // area
        at = component * (tall * wide) + band * (BAND * wide) + wheres[d] % area
        picks.append(at)
    picks = jnp.take(flat, jnp.concatenate(picks), axis=1, mode="clip")
    picks = picks.reshape(group, n, slots).transpose(1, 0, 2)

    live_slots = (jnp.arange(slots, dtype=jnp.int32) < obs_count[0, 0]).astype(jnp.float32)
    taper = 1.0 - loc_index[0, 0].astype(jnp.float32) / 16.0
    weight = obs_precision[0, 0] * (taper * taper) * live_slots

    vmem = pl.BlockSpec(memory_space=pltpu.VMEM)
    dma = pltpu.SemaphoreType.DMA
    out = pl.pallas_call(
        functools.partial(analysis_kernel, n),
        out_shape=jax.ShapeDtypeStruct(cells.shape, jnp.bfloat16),
        in_specs=[vmem] * 4,
        out_specs=vmem,
        scratch_shapes=[
            pltpu.VMEM(picks.shape, jnp.bfloat16),
            pltpu.VMEM(cells.shape, jnp.bfloat16),
            pltpu.VMEM(cells.shape, jnp.bfloat16),
            pltpu.VMEM((2, n * group, n * group), jnp.bfloat16),
        ]
        + [dma((n,))] * 6,
        compiler_params=pltpu.CompilerParams(collective_id=0, has_side_effects=True),
    )(picks, cells, observed_values[0], weight[None])
    out = out.reshape(n, group, 3, BAND, strip).transpose(1, 2, 0, 3, 4)
    return out.reshape(sample_collection.shape)


def solution(mesh):
    in_specs = (
        P("mem", None, None, None, "lon"),
        P(None, None, "lon"),
        P("mem", "lon", None),
        P("mem", "lon", None),
        P("mem", "lon", None),
        P("mem", "lon", None),
        P("mem", "lon"),
    )
    out_specs = P("mem", None, None, None, "lon")
    return jax.shard_map(
        on_device, mesh=mesh, in_specs=in_specs, out_specs=out_specs, check_vma=False
    )
```

time: 121 us -> 94.6 us (0.78)
  the two profiles are of different devices: /device:TPU:0 before, /device:TPU:11 now
where the time goes in v1:
time: 94.6 us; the launch traced here: 93 us
  Pallas kernels  44.3 us (47%)
  local copies, waits for them, and re-layouts  26.4 us (28%)
  starting transfers between devices  9.93 us (10%)
  other arithmetic  7.45 us (8%)
  waiting for transfers between devices  3.99 us (4%)
    pallas_call x1, Pallas kernels, on_device(): pl.pallas_call(functools.partial(analysis_kernel, n), out_shape=jax.Shape...  44.3 us
    gather x1, local copies, waits for them, and re-layouts, on_device(): picks = jnp.take(flat, jnp.concatenate(picks), axis=1, mode='clip')  8.05 us
    ppermute x2, starting transfers between devices, extended_lon(): before = lax.ppermute(value[..., length - width:], 'lon', up)  5.25 us
    ppermute x3, starting transfers between devices, on_device(): wheres.append(lax.ppermute(obs_where[0, 0], 'mem', pairs))  4.67 us
    unnamed x13, local copies, waits for them, and re-layouts  4.33 us
    slice x2, local copies, waits for them, and re-layouts, extended_lon(): before = lax.ppermute(value[..., length - width:], 'lon', up)  2.52 us
    sub x2, other arithmetic, advance(): height[..., 1:-1]  2.3 us
    ppermute x2, waiting for transfers between devices, extended_lon(): before = lax.ppermute(value[..., length - width:], 'lon', up)  2.26 us
  transfers between devices with their start and end apart: 7, of which 2 were waited for; matrix products, arithmetic and copies ran while one was open for 6% of the time, Pallas kernels for 0%

profile of v1, /device:TPU:11, one launch (start us, length us, event | category | flops | bytes accessed | tf_op | source)
XLA Modules:
  0.0 93.0 jit_solution(5350037639461505048)
XLA Ops:
  0.2 2.3 %collective-permute-start.5 = (s32[512]{0:T(512)}, s32[512]{0:T(512)S(1)}, u32[]{:S(2)}, u32[]{:S(2)}) collective-permute-start(s32[512]{0:T(512)} %bitcast.43), channel_id=1, source_target_pairs={{2,0},{3,1},{0,2},{1,3},{6,4},{7,5},{4,6},{5,7},{10,8},{11,9},{8,1... | collective-permute-start | bytes 6152 | tf_op jit(solution)/shard_map/ppermute | solution.py:181
  2.5 2.2 %collective-permute-start.6 = (s32[512]{0:T(512)}, s32[512]{0:T(512)S(1)}, u32[]{:S(2)}, u32[]{:S(2)}) collective-permute-start(s32[512]{0:T(512)} %bitcast.44), channel_id=1, source_target_pairs={{3,0},{0,1},{1,2},{2,3},{7,4},{4,5},{5,6},{6,7},{11,8},{8,9},{9,10... | collective-permute-start | bytes 6152 | tf_op jit(solution)/shard_map/ppermute | solution.py:181
  4.7 0.8 fusion.37
  5.5 2.6 %collective-permute-start.2 = (f32[1,16,8]{2,1,0:T(8,128)S(1)}, f32[1,16,8]{2,1,0:T(8,128)S(1)}, u32[]{:S(2)}, u32[]{:S(2)}) collective-permute-start(f32[1,16,8]{2,1,0:T(8,128)S(1)} %get-tuple-element.28), channel_id=1, source_target_pairs={{0,4},{4,8},{8,12},{12,16},{16,20},{20,24},{24,28},{28,0},{1,5},{5... | collective-permute-start | bytes 1544 | tf_op jit(solution)/shard_map/ppermute | solution.py:62
  8.1 1.7 %fusion.36 = (bf16[64,3,1,16,8]{4,3,2,1,0:T(8,128)(2,1)S(1)}, bf16[64,3,1,16,8]{4,3,2,1,0:T(8,128)(2,1)S(1)}) fusion(bf16[64,3,1,16,128]{4,3,2,1,0:T(8,128)(2,1)} %param.7), kind=kLoop, calls=%fused_computation.83 | loop fusion | bytes 196608 | tf_op jit(solution)/shard_map/slice | solution.py:62
  9.9 0.6 copy.33
  10.5 0.6 copy.34
  12.4 2.6 %collective-permute-start = (bf16[64,3,1,16,8]{0,4,3,2,1:T(8,128)(2,1)S(1)}, bf16[64,3,1,16,8]{0,4,3,2,1:T(8,128)(2,1)S(1)}, u32[]{:S(2)}, u32[]{:S(2)}) collective-permute-start(bf16[64,3,1,16,8]{0,4,3,2,1:T(8,128)(2,1)S(1)} %copy.33), channel_id=1, source_target_pairs={{0,4},{4,8},{8,12},{12,16},{16,20},{20,24},{24,28},{28,0},{1,5},{5... | collective-permute-start | bytes 147464 | tf_op jit(solution)/shard_map/ppermute | solution.py:62
  15.4 2.3 %collective-permute-done = bf16[64,3,1,16,8]{0,4,3,2,1:T(8,128)(2,1)S(1)} collective-permute-done((bf16[64,3,1,16,8]{0,4,3,2,1:T(8,128)(2,1)S(1)}, bf16[64,3,1,16,8]{0,4,3,2,1:T(8,128)(2,1)S(1)}, u32[]{:S(2)}, u32[]{:S(2)}) %collective-permute-start) | collective-permute-done | bytes 49184 | tf_op jit(solution)/shard_map/ppermute | solution.py:62
  18.3 1.7 %collective-permute-done.1 = bf16[64,3,1,16,8]{0,4,3,2,1:T(8,128)(2,1)S(1)} collective-permute-done((bf16[64,3,1,16,8]{0,4,3,2,1:T(8,128)(2,1)S(1)}, bf16[64,3,1,16,8]{0,4,3,2,1:T(8,128)(2,1)S(1)}, u32[]{:S(2)}, u32[]{:S(2)}) %collective-permute-start.1) | collective-permute-done | bytes 49184 | tf_op jit(solution)/shard_map/ppermute | solution.py:63
  20.0 0.6 copy.23
  20.6 0.9 maximum_convert_fusion
  22.4 1.2 %fusion.24 = f32[64,1,16,142]{3,2,0,1:T(8,128)S(1)} fusion(f32[64,1,16,144]{3,2,0,1:T(8,128)S(1)} %get-tuple-element.25, f32[64,1,16,144]{3,2,0,1:T(8,128)S(1)} %get-tuple-element.24, f32[64,1,16,144]{3,2,0,1:T(8,128)S(1)} %get-tuple-element.9, f32[64,1,16,144]{3,2,0,1:T(8,128)S(1)} %get-tuple-element.12), kind=kLoop, calls=%fused_computation.43 | loop fusion | flops 1017856 | bytes 3489792 | tf_op jit(solution)/shard_map/sub | solution.py:42
  23.9 1.4 %broadcast_multiply_fusion.1 = (f32[64,1,16,140]{3,2,0,1:T(8,128)S(1)}, f32[64,1,16,140]{3,2,0,1:T(8,128)S(1)}, f32[64,1,16,140]{3,2,0,1:T(8,128)S(1)}, f32[64,1,16,140]{3,2,0,1:T(8,128)S(1)}) fusion(f32[16,140]{1,0:T(8,128)S(1)} %slice_bitcast_fusion.3, f32[64,1,16,144]{3,2,0,1:T(8,128)S(1)} %get-tuple-element.11, f32[16]{0:T(128)S(1)} %add_multiply_fusion, ...), kind=kLoop, calls=%fused_computation.51 | loop fusion | flops 1863680 | bytes 5743424 | tf_op jit(solution)/shard_map/mul | solution.py:40
  25.6 1.1 %fusion.12 = f32[64,1,16,138]{3,2,0,1:T(8,128)S(1)} fusion(f32[64,1,16,140]{3,2,0,1:T(8,128)S(1)} %get-tuple-element.21, f32[64,1,16,140]{3,2,0,1:T(8,128)S(1)} %get-tuple-element.20, f32[64,1,16,140]{3,2,0,1:T(8,128)S(1)} %get-tuple-element.5, f32[64,1,16,142]{3,2,0,1:T(8,128)S(1)} %fusion.24), kind=kLoop, calls=%fused_computation.27 | loop fusion | flops 989184 | bytes 3391488 | tf_op jit(solution)/shard_map/sub | solution.py:42
  27.3 1.4 %fusion.8 = (bf16[64,1,16,136]{3,2,0,1:T(8,128)(2,1)S(1)}, bf16[64,1,16,136]{3,2,0,1:T(8,128)(2,1)S(1)}) fusion(f32[64,1,16,138]{3,2,0,1:T(8,128)S(1)} %fusion.12, f32[64,1,16,140]{3,2,0,1:T(8,128)S(1)} %get-tuple-element.15, f32[64,1,16,140]{3,2,0,1:T(8,128)S(1)} %get-tuple-element.6, f32[16]{0:T(128)S(1)} %add_multiply_fusion, ...), kind=kLoop, calls=%fused_computation.21 | loop fusion | flops 1810432 | bytes 3899456 | tf_op jit(solution)/shard_map/convert.1
  29.1 3.0 %copy.37 = bf16[64,3,16,136]{0,3,2,1:T(8,128)(2,1)} copy(bf16[64,3,16,136]{3,2,0,1:T(8,128)(2,1)S(1)} %pad_maximum_fusion) | data formatting | bytes 1671168
  32.5 1.9 %pad.24.clone = bf16[64,3,24,136]{0,3,2,1:T(8,128)(2,1)S(1)} pad(bf16[64,3,16,136]{0,3,2,1:T(8,128)(2,1)} %copy.37, bf16[]{:T(256)} %constant.83.clone.1), padding=0_0x0_0x4_4x0_0 | pad | bytes 2088962 | tf_op jit(solution)/shard_map/jit(_pad)/pad | solution.py:195
  34.4 8.1 %gather_fusion = bf16[2048,64]{1,0:T(8,128)(2,1)} fusion(bf16[64,9792]{0,1:T(8,128)(2,1)S(1)} %bitcast.35, s32[2048]{0:T(1024)S(1)} %add_clamp_fusion), kind=kCustom, calls=%fused_computation | custom fusion | bytes 532480 | tf_op jit(solution)/shard_map/jit(_take)/gather | solution.py:205
  42.4 1.9 %copy.28 = bf16[64,4,512]{2,0,1:T(8,128)(2,1)} copy(bf16[64,4,512]{0,2,1:T(8,128)(2,1)} %bitcast.39) | data formatting | bytes 524288 | tf_op jit(solution)/shard_map/reshape | solution.py:206
  44.6 1.2 %reshape.167.cells_ref = bf16[4,64,1536]{2,1,0:T(8,128)(2,1)} reshape(bf16[4,64,3,4,128]{4,3,2,1,0:T(4,128)(2,1)S(1)} %bitcast.37) | data formatting | bytes 1572864 | tf_op jit(solution)/shard_map/reshape | solution.py:193
  45.8 44.3 %shard_map.73 = bf16[4,64,1536]{2,1,0:T(8,128)(2,1)} custom-call(bf16[4,64,512]{2,1,0:T(8,128)(2,1)} %bitcast.40, bf16[4,64,1536]{2,1,0:T(8,128)(2,1)} %reshape.167.cells_ref, f32[1,512]{1,0:T(1,128)} %bitcast.41, f32[1,512]{1,0:T(1,128)} %compare_select_fusion.weight_ref), custom_call_target="tpu_custom_call" | custom-call | tf_op jit(solution)/shard_map/pallas_call | solution.py:214
  90.1 1.8 %reshape.168 = bf16[4,64,3,4,128]{4,3,2,1,0:T(4,128)(2,1)S(1)} reshape(bf16[4,64,1536]{2,1,0:T(8,128)(2,1)} %shard_map.73) | data formatting | bytes 1572864 | tf_op jit(solution)/shard_map/reshape | solution.py:228
  91.8 1.2 %copy.30 = bf16[64,3,4,4,128]{4,3,2,1,0:T(4,128)(2,1)} copy(bf16[64,3,4,4,128]{4,3,1,0,2:T(4,128)(2,1)S(1)} %bitcast.38) | data formatting | bytes 1572864 | tf_op jit(solution)/shard_map/transpose | solution.py:228
  (39 shorter events, 4.7 us)
Async XLA Ops:
  0.0 15.3 %collective-permute-start.4 = (s32[512]{0:T(512)}, s32[512]{0:T(512)S(1)}, u32[]{:S(2)}, u32[]{:S(2)}) collective-permute-start(s32[512]{0:T(512)} %bitcast.42), channel_id=1, source_target_pairs={{1,0},{2,1},{3,2},{0,3},{5,4},{6,5},{7,6},{4,7},{9,8},{10,9},{11,1... | collective-permute-start | bytes 6152 | tf_op jit(solution)/shard_map/ppermute | solution.py:181
  0.2 15.2 %collective-permute-start.5 = (s32[512]{0:T(512)}, s32[512]{0:T(512)S(1)}, u32[]{:S(2)}, u32[]{:S(2)}) collective-permute-start(s32[512]{0:T(512)} %bitcast.43), channel_id=1, source_target_pairs={{2,0},{3,1},{0,2},{1,3},{6,4},{7,5},{4,6},{5,7},{10,8},{11,9},{8,1... | collective-permute-start | bytes 6152 | tf_op jit(solution)/shard_map/ppermute | solution.py:181
  2.5 12.9 %collective-permute-start.6 = (s32[512]{0:T(512)}, s32[512]{0:T(512)S(1)}, u32[]{:S(2)}, u32[]{:S(2)}) collective-permute-start(s32[512]{0:T(512)} %bitcast.44), channel_id=1, source_target_pairs={{3,0},{0,1},{1,2},{2,3},{7,4},{4,5},{5,6},{6,7},{11,8},{8,9},{9,10... | collective-permute-start | bytes 6152 | tf_op jit(solution)/shard_map/ppermute | solution.py:181
  5.5 6.9 %collective-permute-start.2 = (f32[1,16,8]{2,1,0:T(8,128)S(1)}, f32[1,16,8]{2,1,0:T(8,128)S(1)}, u32[]{:S(2)}, u32[]{:S(2)}) collective-permute-start(f32[1,16,8]{2,1,0:T(8,128)S(1)} %get-tuple-element.28), channel_id=1, source_target_pairs={{0,4},{4,8},{8,12},{12,16},{16,20},{20,24},{24,28},{28,0},{1,5},{5... | collective-permute-start | bytes 1544 | tf_op jit(solution)/shard_map/ppermute | solution.py:62
  8.1 6.9 %collective-permute-start.3 = (f32[1,16,8]{2,1,0:T(8,128)S(1)}, f32[1,16,8]{2,1,0:T(8,128)S(1)}, u32[]{:S(2)}, u32[]{:S(2)}) collective-permute-start(f32[1,16,8]{2,1,0:T(8,128)S(1)} %get-tuple-element.29), channel_id=1, source_target_pairs={{4,0},{8,4},{12,8},{16,12},{20,16},{24,20},{28,24},{0,28},{5,1},{9... | collective-permute-start | bytes 1544 | tf_op jit(solution)/shard_map/ppermute | solution.py:63
  9.8 1.3 %copy-start.4 = (s32[1,1,512]{2,1,0:T(1,128)S(1)}, s32[1,1,512]{2,1,0:T(1,128)}, u32[]{:S(2)}) copy-start(s32[1,1,512]{2,1,0:T(1,128)} %param.9) | copy-start | bytes 6148
  9.8 2.0 %copy-start.2 = (f32[1,1,512]{2,1,0:T(1,128)S(1)}, f32[1,1,512]{2,1,0:T(1,128)}, u32[]{:S(2)}) copy-start(f32[1,1,512]{2,1,0:T(1,128)} %param.11) | copy-start | bytes 6148
  9.9 2.0 %copy-start.3 = (s32[1,1,512]{2,1,0:T(1,128)S(1)}, s32[1,1,512]{2,1,0:T(1,128)}, u32[]{:S(2)}) copy-start(s32[1,1,512]{2,1,0:T(1,128)} %param.12) | copy-start | bytes 6148
  9.9 5.2 %copy-start.1 = (f32[1,16,128]{2,1,0:T(8,128)S(1)}, f32[1,16,128]{2,1,0:T(8,128)}, u32[]{:S(2)}) copy-start(f32[1,16,128]{2,1,0:T(8,128)} %param.8) | copy-start | bytes 24580
  10.5 10.1 %copy-start = (bf16[64,3,1,16,128]{4,3,2,1,0:T(8,128)(2,1)S(1)}, bf16[64,3,1,16,128]{4,3,2,1,0:T(8,128)(2,1)}, u32[]{:S(2)}) copy-start(bf16[64,3,1,16,128]{4,3,2,1,0:T(8,128)(2,1)} %param.7) | copy-start | bytes 2359300
  12.4 5.2 %collective-permute-start = (bf16[64,3,1,16,8]{0,4,3,2,1:T(8,128)(2,1)S(1)}, bf16[64,3,1,16,8]{0,4,3,2,1:T(8,128)(2,1)S(1)}, u32[]{:S(2)}, u32[]{:S(2)}) collective-permute-start(bf16[64,3,1,16,8]{0,4,3,2,1:T(8,128)(2,1)S(1)} %copy.33), channel_id=1, source_target_pairs={{0,4},{4,8},{8,12},{12,16},{16,20},{20,24},{24,28},{28,0},{1,5},{5... | collective-permute-start | bytes 147464 | tf_op jit(solution)/shard_map/ppermute | solution.py:62
  15.1 4.9 %collective-permute-start.1 = (bf16[64,3,1,16,8]{0,4,3,2,1:T(8,128)(2,1)S(1)}, bf16[64,3,1,16,8]{0,4,3,2,1:T(8,128)(2,1)S(1)}, u32[]{:S(2)}, u32[]{:S(2)}) collective-permute-start(bf16[64,3,1,16,8]{0,4,3,2,1:T(8,128)(2,1)S(1)} %copy.34), channel_id=1, source_target_pairs={{4,0},{8,4},{12,8},{16,12},{20,16},{24,20},{28,24},{0,28},{5,1},{9... | collective-permute-start | bytes 147464 | tf_op jit(solution)/shard_map/ppermute | solution.py:63

commit v2 on v1

v2 whole, which is shorter than its diff:
```python
import functools
import math

import jax
import jax.numpy as jnp
from jax import lax
from jax.experimental import pallas as pl
from jax.experimental.pallas import tpu as pltpu
from jax.sharding import PartitionSpec as P

STEPS = 2
MARGIN_WIDTH = 4
BAND = 4
NS_ITERS = 5
MESH = pl.DeviceIdType.MESH
HIGHEST = lax.Precision.HIGHEST

time_step = 0.8
inflation = 1.1


LANES = 128
REACH = 2 * STEPS + MARGIN_WIDTH
TILE = 16


def coriolis_rate(shape):
    latitude = lax.broadcasted_iota(jnp.int32, shape, 0).astype(jnp.float32)
    return 0.4 * (latitude / (shape[0] - 1) - 0.5)


def lat_diff(field):
    edge = jnp.zeros_like(field[:1])
    north = jnp.concatenate([field[1:], edge], axis=0)
    south = jnp.concatenate([edge, field[:-1]], axis=0)
    return 0.5 * (north - south)


def shifted(field, shift):
    return pltpu.roll(field, shift % LANES, axis=field.ndim - 1)


def lon_diff(field):
    return 0.5 * (shifted(field, -1) - shifted(field, 1))


def forecast(height, east, north, depth, spin):
    for step_index in range(STEPS):
        height_new = height - time_step * (lon_diff(depth * east) + lat_diff(depth * north))
        east_new = east - time_step * lon_diff(height_new) + time_step * spin * north
        north_new = north - time_step * lat_diff(height_new) - time_step * spin * east
        height, east, north = height_new, east_new, north_new
    return height, east, north


def exchange_order(n):
    return sorted(range(1, n), key=lambda d: (-min(d, n - d), d))


def edge_window(own, west, east, lane):
    value = jnp.where(lane < REACH, west, shifted(own, REACH))
    value = jnp.where(lane >= 2 * REACH, shifted(own, 3 * REACH), value)
    return jnp.where((lane >= 3 * REACH) & (lane < 4 * REACH), east, value)


def analysis_kernel(
    n, x_ref, depth_ref, where_ref, values_ref, precision_ref, loc_ref, count_ref, out_ref,
    halo_out, halo_in, depth_in, wheres, main, edge, picks, picked, cells, result, transform,
    halo_send, halo_recv, depth_send, depth_recv, where_send, where_recv,
    pick_send, pick_recv, cell_send, cell_recv, back_send, back_recv,
):
    me = lax.axis_index("mem")
    lon, strips = lax.axis_index("lon"), lax.axis_size("lon")
    right, left = lax.rem(lon + 1, strips), lax.rem(lon + strips - 1, strips)
    _, rows, group, _ = x_ref.shape
    members = n * group
    slots = values_ref.shape[1]
    per_tile = LANES // REACH
    margin = MARGIN_WIDTH

    barrier = pltpu.get_barrier_semaphore()
    for d in range(1, n):
        pl.semaphore_signal(
            barrier, inc=1, device_id={"mem": lax.rem(me + d, n)}, device_id_type=MESH
        )
    for side in (left, right):
        pl.semaphore_signal(barrier, inc=1, device_id={"lon": side}, device_id_type=MESH)

    lane = lax.broadcasted_iota(jnp.int32, (TILE, LANES), 1)

    @pl.loop(0, 3 * (group // TILE))
    def _(at):
        c, m = at // (group // TILE), pl.ds(pl.multiple_of(at % (group // TILE) * TILE, TILE), TILE)
        for k in range(rows // per_tile):
            first = last = jnp.zeros((TILE, LANES), jnp.float32)
            for r in range(per_tile):
                own = x_ref[c, k * per_tile + r, m, :].astype(jnp.float32)
                here = (lane >= r * REACH) & (lane < (r + 1) * REACH)
                first = jnp.where(here, shifted(own, r * REACH), first)
                last = jnp.where(here, shifted(own, (r + 1) * REACH), last)
            halo_out[0, c, k, m, :] = last.astype(jnp.bfloat16)
            halo_out[1, c, k, m, :] = first.astype(jnp.bfloat16)

    pl.semaphore_wait(barrier, n + 1)

    def send(src, dst, ss, rs, i, peer):
        copy = pltpu.make_async_remote_copy(
            src_ref=src, dst_ref=dst, send_sem=ss.at[i], recv_sem=rs.at[i],
            device_id=peer, device_id_type=MESH,
        )
        copy.start()
        return copy

    order = exchange_order(n)
    halo_copies, where_copies = [], []
    for i, side in enumerate((right, left)):
        peer = {"lon": side}
        halo_copies.append(send(halo_out.at[i], halo_in.at[i], halo_send, halo_recv, i, peer))
        halo_copies.append(send(depth_ref, depth_in.at[i], depth_send, depth_recv, i, peer))
    for d in order:
        peer = {"mem": lax.rem(me + d, n)}
        where_copies.append(send(where_ref, wheres.at[me], where_send, where_recv, d, peer))
    wheres[me] = where_ref[...]

    spin = coriolis_rate((rows, 1, LANES))
    blank = jnp.zeros((margin, TILE, LANES), jnp.bfloat16)

    def group_rows(g):
        return pl.ds(pl.multiple_of(g * TILE, TILE), TILE)

    def put(ref, c, m, value):
        ref[c, pl.ds(0, margin), m, :] = blank
        ref[c, pl.ds(margin, rows), m, :] = value
        ref[c, pl.ds(margin + rows, margin), m, :] = blank

    own_depth = depth_ref[...].reshape(rows, 1, LANES)

    @pl.loop(0, group // TILE)
    def _(g):
        m = group_rows(g)
        fields = forecast(
            *[x_ref[c, :, m, :].astype(jnp.float32) for c in range(3)], own_depth, spin
        )
        for c in range(3):
            put(main, c, m, fields[c].astype(jnp.bfloat16))

    for copy in halo_copies:
        copy.wait()

    lane_row = lax.broadcasted_iota(jnp.int32, (rows, LANES), 1)
    edge_depth = edge_window(
        depth_ref[...],
        shifted(depth_in[0], REACH),
        shifted(depth_in[1], 3 * REACH),
        lane_row,
    ).reshape(rows, 1, LANES)

    @pl.loop(0, group // TILE)
    def _(g):
        m = group_rows(g)
        windows = []
        for c in range(3):
            window = []
            for r in range(rows):
                k, slot = r // per_tile, r % per_tile
                own = x_ref[c, r, m, :].astype(jnp.float32)
                west = shifted(halo_in[0, c, k, m, :].astype(jnp.float32), -slot * REACH)
                east = shifted(halo_in[1, c, k, m, :].astype(jnp.float32), (3 - slot) * REACH)
                window.append(edge_window(own, west, east, lane))
            windows.append(jnp.stack(window))
        fields = forecast(*windows, edge_depth, spin)
        for c in range(3):
            value = fields[c].astype(jnp.bfloat16)
            put(edge, c, m, value)
            value = value.astype(jnp.float32)
            inside = main[c, pl.ds(margin, rows), m, :].astype(jnp.float32)
            inside = jnp.where(lane < 2 * STEPS, shifted(value, -REACH), inside)
            inside = jnp.where(
                lane >= LANES - 2 * STEPS, shifted(value, LANES - 3 * REACH), inside
            )
            main[c, pl.ds(margin, rows), m, :] = inside.astype(jnp.bfloat16)

    def send_cells(d):
        to = lax.rem(me + d, n)
        src = main.at[:, pl.ds(margin + to * BAND, BAND)]
        return send(src, cells.at[me], cell_send, cell_recv, d, {"mem": to})

    ahead = len(order) // 3 if n > 3 else 0
    cell_copies = [send_cells(d) for d in order[:ahead]]
    cells[me] = main[:, pl.ds(margin + me * BAND, BAND)]
    for copy in where_copies:
        copy.wait()

    tall = BAND + 2 * margin
    place = lax.broadcasted_iota(jnp.int32, (LANES, slots), 0)

    def pick(band):
        rank, column = wheres[band, 0:1, :], wheres[band, 1:2, :]
        border = jnp.where(column < margin, column + REACH - margin, -1)
        border = jnp.where(
            column >= LANES + margin, column - (LANES + margin) + 3 * REACH, border
        )
        chosen = jnp.concatenate([place == column - margin, place == border], axis=0)
        chosen = jnp.where(chosen, 1.0, 0.0).astype(jnp.bfloat16)
        total = jnp.zeros((group, slots), jnp.float32)
        for c in range(3):
            span = pl.ds(band * BAND, tall)
            area = jnp.concatenate([main[c, span], edge[c, span]], axis=-1)
            at_columns = jnp.dot(
                area.reshape(tall * group, 2 * LANES), chosen, preferred_element_type=jnp.float32
            )
            for r in range(tall):
                part = at_columns[r * group : (r + 1) * group]
                total = jnp.where(rank == c * tall + r, part, total)
        return total.astype(jnp.bfloat16)

    pick_copies = []
    for d in order:
        to = lax.rem(me + d, n)
        picks[d] = pick(to)
        pick_copies.append(
            send(picks.at[d], picked.at[me], pick_send, pick_recv, d, {"mem": to})
        )
    cell_copies += [send_cells(d) for d in order[ahead:]]
    picked[me] = pick(me)
    for copy in pick_copies:
        copy.wait()

    taper = 1.0 - loc_ref[...].astype(jnp.float32) / 16.0
    slot_at = lax.broadcasted_iota(jnp.int32, (1, slots), 1)
    weight = jnp.where(slot_at < count_ref[...], precision_ref[...] * (taper * taper), 0.0)
    obs = picked[...].astype(jnp.float32).reshape(members, slots)
    obs_mean = jnp.mean(obs, axis=0, keepdims=True)
    spread = obs - obs_mean
    weighted = spread * weight
    innovation = values_ref[...] - obs_mean

    def mm(a, b):
        return jnp.dot(a, b, precision=HIGHEST, preferred_element_type=jnp.float32)

    gram = lax.dot_general(
        weighted, spread, (((1,), (1,)), ((), ())),
        precision=HIGHEST, preferred_element_type=jnp.float32,
    )
    drive = jnp.sum(weighted * innovation, axis=1, keepdims=True)
    prior = (members - 1) / inflation
    trace = jnp.sum(jnp.sum(weighted * spread, axis=1, keepdims=True), axis=0, keepdims=True)
    trace_bound = prior + trace
    row_at = lax.broadcasted_iota(jnp.int32, (members, members), 0)
    column_at = lax.broadcasted_iota(jnp.int32, (members, members), 1)
    identity = jnp.where(row_at == column_at, 1.0, 0.0).astype(jnp.float32)
    root_iter = (gram + prior * identity) / trace_bound
    correction = 1.5 * identity - 0.5 * root_iter
    root_iter = mm(root_iter, correction)
    inv_root = correction
    for sweep in range(1, NS_ITERS):
        correction = 1.5 * identity - 0.5 * mm(inv_root, root_iter)
        if sweep < NS_ITERS - 1:
            root_iter = mm(root_iter, correction)
        inv_root = mm(correction, inv_root)
    shrink = inv_root * lax.rsqrt(trace_bound)
    inner = jnp.sum(shrink * drive, axis=0, keepdims=True)
    mean_weight = jnp.sum(shrink * inner, axis=1, keepdims=True)
    weights = math.sqrt(members - 1) * shrink + mean_weight
    weights = weights + (1.0 - jnp.sum(weights, axis=0, keepdims=True)) / members
    weights_t = weights.T
    high = weights_t.astype(jnp.bfloat16)
    transform[0] = high
    transform[1] = (weights_t - high.astype(jnp.float32)).astype(jnp.bfloat16)

    for copy in cell_copies:
        copy.wait()
    all_cells = jnp.concatenate(
        [cells[:, c, r].reshape(members, LANES) for c in range(3) for r in range(BAND)], axis=1
    )

    def analysed(peer):
        rows = pl.ds(pl.multiple_of(peer * group, group), group)
        total = jnp.dot(transform[0, rows, :], all_cells, preferred_element_type=jnp.float32)
        total += jnp.dot(transform[1, rows, :], all_cells, preferred_element_type=jnp.float32)
        return total.astype(jnp.bfloat16)

    def store(ref, at, value):
        for c in range(3):
            for r in range(BAND):
                start = (c * BAND + r) * LANES
                ref[at, c, r] = value[:, start : start + LANES]

    back_copies = []
    for d in order:
        peer = lax.rem(me + d, n)
        store(result, d, analysed(peer))
        back_copies.append(
            send(result.at[d], out_ref.at[me], back_send, back_recv, d, {"mem": peer})
        )
    store(out_ref, me, analysed(me))
    for copy in back_copies:
        copy.wait()


def on_device(
    sample_collection, layer_depth, obs_where, observed_values, obs_precision, loc_index, obs_count
):
    n = lax.axis_size("mem")
    group, _, _, rows, strip = sample_collection.shape
    slots = obs_where.shape[-1]
    wide = strip + 2 * MARGIN_WIDTH
    x = sample_collection[:, :, 0].transpose(1, 2, 0, 3)
    where = jnp.stack([obs_where[0, 0] // wide, obs_where[0, 0] % wide])
    vmem = pl.BlockSpec(memory_space=pltpu.VMEM)
    dma = pltpu.SemaphoreType.DMA
    bf16 = jnp.bfloat16
    halo = (2, 3, rows // (LANES // REACH), group, LANES)
    padded = (3, rows + 2 * MARGIN_WIDTH, group, LANES)
    block = (n, 3, BAND, group, LANES)
    out = pl.pallas_call(
        functools.partial(analysis_kernel, n),
        out_shape=jax.ShapeDtypeStruct(block, bf16),
        in_specs=[vmem] * 7,
        out_specs=vmem,
        scratch_shapes=[
            pltpu.VMEM(halo, bf16),
            pltpu.VMEM(halo, bf16),
            pltpu.VMEM((2, rows, LANES), jnp.float32),
            pltpu.VMEM((n, 2, slots), jnp.int32),
            pltpu.VMEM(padded, bf16),
            pltpu.VMEM(padded, bf16),
            pltpu.VMEM((n, group, slots), bf16),
            pltpu.VMEM((n, group, slots), bf16),
            pltpu.VMEM(block, bf16),
            pltpu.VMEM(block, bf16),
            pltpu.VMEM((2, n * group, n * group), bf16),
        ]
        + [dma((2,))] * 4
        + [dma((n,))] * 8,
        compiler_params=pltpu.CompilerParams(collective_id=0, has_side_effects=True),
    )(x, layer_depth[0], where, observed_values[0], obs_precision[0], loc_index[0], obs_count)
    out = out.transpose(3, 1, 0, 2, 4)
    return out.reshape(sample_collection.shape)


def solution(mesh):
    in_specs = (
        P("mem", None, None, None, "lon"),
        P(None, None, "lon"),
        P("mem", "lon", None),
        P("mem", "lon", None),
        P("mem", "lon", None),
        P("mem", "lon", None),
        P("mem", "lon"),
    )
    out_specs = P("mem", None, None, None, "lon")
    return jax.shard_map(
        on_device, mesh=mesh, in_specs=in_specs, out_specs=out_specs, check_vma=False
    )
```

time: 94.6 us -> 65.7 us (0.69)
  the two profiles are of different devices: /device:TPU:11 before, /device:TPU:20 now
where the time goes in v2:
time: 65.7 us; the launch traced here: 65.5 us
  Pallas kernels  58.7 us (89%)
  local copies, waits for them, and re-layouts  5.47 us (8%)
  between operations  0.68 us (1%)
    pallas_call x1, Pallas kernels, on_device(): pl.pallas_call(functools.partial(analysis_kernel, n), out_shape=jax.Shape...  58.7 us
    unnamed x3, local copies, waits for them, and re-layouts  2.89 us
    reshape x1, local copies, waits for them, and re-layouts, on_device(): return out.reshape(sample_collection.shape)  1.39 us

profile of v2, /device:TPU:20, one launch (start us, length us, event | category | flops | bytes accessed | tf_op | source)
XLA Modules:
  0.0 65.5 jit_solution(6381918306392083788)
XLA Ops:
  0.7 0.0 copy-start
  0.7 0.7 %copy-done = s32[1,1,512]{2,1,0:T(1,128)S(1)} copy-done((s32[1,1,512]{2,1,0:T(1,128)S(1)}, s32[1,1,512]{2,1,0:T(1,128)}, u32[]{:S(2)}) %copy-start) | copy-done | bytes 2072
  1.4 0.6 pad_add_fusion.where_ref
  2.0 2.2 %copy.13 = bf16[64,3,1,16,128]{4,0,3,1,2:T(8,128)(2,1)} copy(bf16[64,3,1,16,128]{4,3,2,1,0:T(8,128)(2,1)} %param.7) | data formatting | bytes 1572864 | tf_op args[0]
  4.2 58.7 %shard_map.73 = bf16[4,3,4,64,128]{4,3,2,1,0:T(8,128)(2,1)} custom-call(bf16[3,16,64,128]{3,2,1,0:T(8,128)(2,1)} %bitcast.21, f32[16,128]{1,0:T(8,128)} %bitcast.23, s32[2,512]{1,0:T(2,128)} %pad_add_fusion.where_ref, f32[1,512]{1,0:T(1,128)} %bitcast.24, f32[1,512]{1,0:T(1,128)} %bitcast.25, s32[1,512]{1,0:T(1,128)} %bitcast.26, s32[1,1]{1,0:T(1,128)S(6)} %copy.14.count_ref), custom_call_target="tpu_custom_call" | custom-call | tf_op jit(solution)/shard_map/pallas_call | solution.py:316
  62.9 1.2 %copy.10 = bf16[64,3,4,4,128]{4,0,3,2,1:T(8,128)(2,1)S(1)} copy(bf16[64,3,4,4,128]{4,0,3,1,2:T(8,128)(2,1)} %bitcast.20) | data formatting | bytes 1572864 | tf_op jit(solution)/shard_map/transpose | solution.py:338
  64.1 1.4 %copy.11 = bf16[64,3,1,16,128]{4,3,2,1,0:T(8,128)(2,1)} copy(bf16[64,3,1,16,128]{4,0,3,1,2:T(8,128)(2,1)S(1)} %bitcast.22) | data formatting | bytes 1572864 | tf_op jit(solution)/shard_map/reshape | solution.py:339
  (1 shorter events, 0.0 us)
Async XLA Ops:
  0.7 0.7 %copy-start = (s32[1,1,512]{2,1,0:T(1,128)S(1)}, s32[1,1,512]{2,1,0:T(1,128)}, u32[]{:S(2)}) copy-start(s32[1,1,512]{2,1,0:T(1,128)} %param.9) | copy-start | bytes 6148

commit v3 on v2

--- a/solution.py
+++ b/solution.py
@@ -65,9 +65,9 @@
 
 def analysis_kernel(
     n, x_ref, depth_ref, where_ref, values_ref, precision_ref, loc_ref, count_ref, out_ref,
-    halo_out, halo_in, depth_in, wheres, main, edge, picks, picked, cells, result, transform,
+    halo_out, halo_in, depth_in, wheres, main, fixed, edge, border_out, border_in, picks, picked, cells, result, transform,
     halo_send, halo_recv, depth_send, depth_recv, where_send, where_recv,
-    pick_send, pick_recv, cell_send, cell_recv, back_send, back_recv,
+    border_send, border_recv, pick_send, pick_recv, cell_send, cell_recv, back_send, back_recv,
 ):
     me = lax.axis_index("mem")
     lon, strips = lax.axis_index("lon"), lax.axis_size("lon")
@@ -101,6 +101,28 @@
             halo_out[0, c, k, m, :] = last.astype(jnp.bfloat16)
             halo_out[1, c, k, m, :] = first.astype(jnp.bfloat16)
 
+    spin = coriolis_rate((rows, 1, LANES))
+    blank = jnp.zeros((margin, TILE, LANES), jnp.bfloat16)
+
+    def group_rows(g):
+        return pl.ds(pl.multiple_of(g * TILE, TILE), TILE)
+
+    def put(ref, c, m, value):
+        ref[c, pl.ds(0, margin), m, :] = blank
+        ref[c, pl.ds(margin, rows), m, :] = value
+        ref[c, pl.ds(margin + rows, margin), m, :] = blank
+
+    own_depth = depth_ref[...].reshape(rows, 1, LANES)
+
+    @pl.loop(0, group // TILE)
+    def _(g):
+        m = group_rows(g)
+        fields = forecast(
+            *[x_ref[c, :, m, :].astype(jnp.float32) for c in range(3)], own_depth, spin
+        )
+        for c in range(3):
+            main[c, :, m, :] = fields[c].astype(jnp.bfloat16)
+
     pl.semaphore_wait(barrier, n + 1)
 
     def send(src, dst, ss, rs, i, peer):
@@ -122,27 +144,13 @@
         where_copies.append(send(where_ref, wheres.at[me], where_send, where_recv, d, peer))
     wheres[me] = where_ref[...]
 
-    spin = coriolis_rate((rows, 1, LANES))
-    blank = jnp.zeros((margin, TILE, LANES), jnp.bfloat16)
-
-    def group_rows(g):
-        return pl.ds(pl.multiple_of(g * TILE, TILE), TILE)
-
-    def put(ref, c, m, value):
-        ref[c, pl.ds(0, margin), m, :] = blank
-        ref[c, pl.ds(margin, rows), m, :] = value
-        ref[c, pl.ds(margin + rows, margin), m, :] = blank
-
-    own_depth = depth_ref[...].reshape(rows, 1, LANES)
-
-    @pl.loop(0, group // TILE)
-    def _(g):
-        m = group_rows(g)
-        fields = forecast(
-            *[x_ref[c, :, m, :].astype(jnp.float32) for c in range(3)], own_depth, spin
-        )
-        for c in range(3):
-            put(main, c, m, fields[c].astype(jnp.bfloat16))
+    def send_cells(d, ref, skip):
+        to = lax.rem(me + d, n)
+        src = ref.at[:, pl.ds(to * BAND + skip, BAND)]
+        return send(src, cells.at[me], cell_send, cell_recv, d, {"mem": to})
+
+    early, late = order[:-1], order[-1:]
+    cell_copies = [send_cells(d, main, 0) for d in early]
 
     for copy in halo_copies:
         copy.wait()
@@ -173,21 +181,37 @@
             value = fields[c].astype(jnp.bfloat16)
             put(edge, c, m, value)
             value = value.astype(jnp.float32)
-            inside = main[c, pl.ds(margin, rows), m, :].astype(jnp.float32)
+            inside = main[c, :, m, :].astype(jnp.float32)
             inside = jnp.where(lane < 2 * STEPS, shifted(value, -REACH), inside)
             inside = jnp.where(
                 lane >= LANES - 2 * STEPS, shifted(value, LANES - 3 * REACH), inside
             )
-            main[c, pl.ds(margin, rows), m, :] = inside.astype(jnp.bfloat16)
-
-    def send_cells(d):
-        to = lax.rem(me + d, n)
-        src = main.at[:, pl.ds(margin + to * BAND, BAND)]
-        return send(src, cells.at[me], cell_send, cell_recv, d, {"mem": to})
-
-    ahead = len(order) // 3 if n > 3 else 0
-    cell_copies = [send_cells(d) for d in order[:ahead]]
-    cells[me] = main[:, pl.ds(margin + me * BAND, BAND)]
+            put(fixed, c, m, inside.astype(jnp.bfloat16))
+
+    cells[me] = fixed[:, pl.ds(margin + me * BAND, BAND)]
+
+    @pl.loop(0, group // TILE)
+    def _(g):
+        m = group_rows(g)
+        for i, d in enumerate(early):
+            to = lax.rem(me + d, n)
+            packed = jnp.zeros((TILE, LANES), jnp.float32)
+            for c in range(3):
+                for r in range(BAND):
+                    start = (c * BAND + r) * REACH
+                    part = edge[c, margin + to * BAND + r, m, :].astype(jnp.float32)
+                    west = (lane >= start) & (lane < start + 2 * STEPS)
+                    east = (lane >= start + 2 * STEPS) & (lane < start + REACH)
+                    packed = jnp.where(west, shifted(part, start - REACH), packed)
+                    moved = shifted(part, start + 4 * STEPS - 3 * REACH)
+                    packed = jnp.where(east, moved, packed)
+            border_out[i, m, :] = packed.astype(jnp.bfloat16)
+
+    border_copies = [
+        send(border_out.at[i], border_in.at[i], border_send, border_recv, i,
+             {"mem": lax.rem(me + d, n)})
+        for i, d in enumerate(early)
+    ]
     for copy in where_copies:
         copy.wait()
 
@@ -195,7 +219,9 @@
     place = lax.broadcasted_iota(jnp.int32, (LANES, slots), 0)
 
     def pick(band):
-        rank, column = wheres[band, 0:1, :], wheres[band, 1:2, :]
+        where = wheres[band].astype(jnp.float32)
+        rank = jnp.floor((where + 0.5) * (1.0 / (LANES + 2 * margin)))
+        column = (where - rank * (LANES + 2 * margin)).astype(jnp.int32)
         border = jnp.where(column < margin, column + REACH - margin, -1)
         border = jnp.where(
             column >= LANES + margin, column - (LANES + margin) + 3 * REACH, border
@@ -205,13 +231,13 @@
         total = jnp.zeros((group, slots), jnp.float32)
         for c in range(3):
             span = pl.ds(band * BAND, tall)
-            area = jnp.concatenate([main[c, span], edge[c, span]], axis=-1)
+            area = jnp.concatenate([fixed[c, span], edge[c, span]], axis=-1)
             at_columns = jnp.dot(
                 area.reshape(tall * group, 2 * LANES), chosen, preferred_element_type=jnp.float32
             )
             for r in range(tall):
                 part = at_columns[r * group : (r + 1) * group]
-                total = jnp.where(rank == c * tall + r, part, total)
+                total = jnp.where(rank == float(c * tall + r), part, total)
         return total.astype(jnp.bfloat16)
 
     pick_copies = []
@@ -221,8 +247,26 @@
         pick_copies.append(
             send(picks.at[d], picked.at[me], pick_send, pick_recv, d, {"mem": to})
         )
-    cell_copies += [send_cells(d) for d in order[ahead:]]
+    late_copies = [send_cells(d, fixed, margin) for d in late]
     picked[me] = pick(me)
+    for copy in cell_copies + border_copies:
+        copy.wait()
+
+    @pl.loop(0, group // TILE)
+    def _(g):
+        m = group_rows(g)
+        for i, d in enumerate(early):
+            source = lax.rem(me + n - d, n)
+            packed = border_in[i, m, :].astype(jnp.float32)
+            for c in range(3):
+                for r in range(BAND):
+                    start = (c * BAND + r) * REACH
+                    value = cells[source, c, r, m, :].astype(jnp.float32)
+                    value = jnp.where(lane < 2 * STEPS, shifted(packed, -start), value)
+                    moved = shifted(packed, LANES - start - 4 * STEPS)
+                    value = jnp.where(lane >= LANES - 2 * STEPS, moved, value)
+                    cells[source, c, r, m, :] = value.astype(jnp.bfloat16)
+
     for copy in pick_copies:
         copy.wait()
 
@@ -268,7 +312,7 @@
     transform[0] = high
     transform[1] = (weights_t - high.astype(jnp.float32)).astype(jnp.bfloat16)
 
-    for copy in cell_copies:
+    for copy in late_copies:
         copy.wait()
     all_cells = jnp.concatenate(
         [cells[:, c, r].reshape(members, LANES) for c in range(3) for r in range(BAND)], axis=1
@@ -280,20 +324,22 @@
         total += jnp.dot(transform[1, rows, :], all_cells, preferred_element_type=jnp.float32)
         return total.astype(jnp.bfloat16)
 
-    def store(ref, at, value):
+    def slabs(value):
         for c in range(3):
             for r in range(BAND):
                 start = (c * BAND + r) * LANES
-                ref[at, c, r] = value[:, start : start + LANES]
+                yield c, r, value[:, start : start + LANES]
 
     back_copies = []
     for d in order:
         peer = lax.rem(me + d, n)
-        store(result, d, analysed(peer))
+        for c, r, value in slabs(analysed(peer)):
+            result[d, c, r] = value
         back_copies.append(
-            send(result.at[d], out_ref.at[me], back_send, back_recv, d, {"mem": peer})
-        )
-    store(out_ref, me, analysed(me))
+            send(result.at[d], out_ref.at[:, pl.ds(me * BAND, BAND)], back_send, back_recv, d, {"mem": peer})
+        )
+    for c, r, value in slabs(analysed(me)):
+        out_ref[c, me * BAND + r] = value
     for copy in back_copies:
         copy.wait()
 
@@ -304,9 +350,7 @@
     n = lax.axis_size("mem")
     group, _, _, rows, strip = sample_collection.shape
     slots = obs_where.shape[-1]
-    wide = strip + 2 * MARGIN_WIDTH
     x = sample_collection[:, :, 0].transpose(1, 2, 0, 3)
-    where = jnp.stack([obs_where[0, 0] // wide, obs_where[0, 0] % wide])
     vmem = pl.BlockSpec(memory_space=pltpu.VMEM)
     dma = pltpu.SemaphoreType.DMA
     bf16 = jnp.bfloat16
@@ -315,16 +359,19 @@
     block = (n, 3, BAND, group, LANES)
     out = pl.pallas_call(
         functools.partial(analysis_kernel, n),
-        out_shape=jax.ShapeDtypeStruct(block, bf16),
+        out_shape=jax.ShapeDtypeStruct((3, rows, group, LANES), bf16),
         in_specs=[vmem] * 7,
         out_specs=vmem,
         scratch_shapes=[
             pltpu.VMEM(halo, bf16),
             pltpu.VMEM(halo, bf16),
             pltpu.VMEM((2, rows, LANES), jnp.float32),
-            pltpu.VMEM((n, 2, slots), jnp.int32),
+            pltpu.VMEM((n, 1, slots), jnp.int32),
+            pltpu.VMEM((3, rows, group, LANES), bf16),
             pltpu.VMEM(padded, bf16),
             pltpu.VMEM(padded, bf16),
+            pltpu.VMEM((n, group, LANES), bf16),
+            pltpu.VMEM((n, group, LANES), bf16),
             pltpu.VMEM((n, group, slots), bf16),
             pltpu.VMEM((n, group, slots), bf16),
             pltpu.VMEM(block, bf16),
@@ -332,10 +379,10 @@
             pltpu.VMEM((2, n * group, n * group), bf16),
         ]
         + [dma((2,))] * 4
-        + [dma((n,))] * 8,
+        + [dma((n,))] * 10,
         compiler_params=pltpu.CompilerParams(collective_id=0, has_side_effects=True),
-    )(x, layer_depth[0], where, observed_values[0], obs_precision[0], loc_index[0], obs_count)
-    out = out.transpose(3, 1, 0, 2, 4)
+    )(x, layer_depth[0], obs_where[0], observed_values[0], obs_precision[0], loc_index[0], obs_count)
+    out = out.transpose(2, 0, 1, 3)
     return out.reshape(sample_collection.shape)
 
 

time: 65.7 us -> 61.4 us (0.935)
  the two profiles are of different devices: /device:TPU:20 before, /device:TPU:11 now
where the time goes in v3:
time: 61.4 us; the launch traced here: 61.2 us
  Pallas kernels  55.8 us (91%)
  local copies, waits for them, and re-layouts  4.74 us (8%)
  between operations  0.66 us (1%)
    pallas_call x1, Pallas kernels, on_device(): pl.pallas_call(functools.partial(analysis_kernel, n), out_shape=jax.Shape...  55.8 us
    reshape x1, local copies, waits for them, and re-layouts, on_device(): return out.reshape(sample_collection.shape)  2.52 us
    unnamed x1, local copies, waits for them, and re-layouts  2.22 us

profile of v3, /device:TPU:11, one launch (start us, length us, event | category | flops | bytes accessed | tf_op | source)
XLA Modules:
  0.0 61.2 jit_solution(1297276539580208200)
XLA Ops:
  0.7 2.2 %copy.11 = bf16[64,3,1,16,128]{4,0,3,1,2:T(8,128)(2,1)} copy(bf16[64,3,1,16,128]{4,3,2,1,0:T(8,128)(2,1)} %param.7) | data formatting | bytes 1572864 | tf_op args[0]
  2.9 55.8 %shard_map.73 = bf16[3,16,64,128]{3,2,1,0:T(8,128)(2,1)} custom-call(bf16[3,16,64,128]{3,2,1,0:T(8,128)(2,1)} %bitcast.14, f32[16,128]{1,0:T(8,128)} %bitcast.15, s32[1,512]{1,0:T(1,128)} %bitcast.16, f32[1,512]{1,0:T(1,128)} %bitcast.17, f32[1,512]{1,0:T(1,128)} %bitcast.18, s32[1,512]{1,0:T(1,128)} %bitcast.19, s32[1,1]{1,0:T(1,128)S(6)} %copy.12.count_ref), custom_call_target="tpu_custom_call" | custom-call | tf_op jit(solution)/shard_map/pallas_call | solution.py:360
  58.7 2.5 %copy.9 = bf16[64,3,1,16,128]{4,3,2,1,0:T(8,128)(2,1)} copy(bf16[64,3,1,16,128]{4,0,3,1,2:T(8,128)(2,1)} %bitcast.13) | data formatting | bytes 1572864 | tf_op jit(solution)/shard_map/reshape | solution.py:386

commit v4 on v3

--- a/solution.py
+++ b/solution.py
@@ -149,7 +149,7 @@
         src = ref.at[:, pl.ds(to * BAND + skip, BAND)]
         return send(src, cells.at[me], cell_send, cell_recv, d, {"mem": to})
 
-    early, late = order[:-1], order[-1:]
+    early, late = order[:-2], order[-2:]
     cell_copies = [send_cells(d, main, 0) for d in early]
 
     for copy in halo_copies:
@@ -279,8 +279,15 @@
     weighted = spread * weight
     innovation = values_ref[...] - obs_mean
 
+    def split(a):
+        high = a.astype(jnp.bfloat16)
+        return high, (a - high.astype(jnp.float32)).astype(jnp.bfloat16)
+
     def mm(a, b):
-        return jnp.dot(a, b, precision=HIGHEST, preferred_element_type=jnp.float32)
+        (ah, al), (bh, bl) = split(a), split(b)
+        total = jnp.dot(ah, bl, preferred_element_type=jnp.float32)
+        total += jnp.dot(al, bh, preferred_element_type=jnp.float32)
+        return total + jnp.dot(ah, bh, preferred_element_type=jnp.float32)
 
     gram = lax.dot_general(
         weighted, spread, (((1,), (1,)), ((), ())),

time: 61.4 us -> 55.6 us (0.906)
  Pallas kernels: 55.8 us -> 50 us
    pallas_call x1, Pallas kernels: 55.8 us -> 50 us  [on_device(): pl.pallas_call(functools.partial(analysis_kernel, n), out_shape=jax.Shape...]
where the time goes in v4:
time: 55.6 us; the launch traced here: 55.4 us
  Pallas kernels  50 us (90%)
  local copies, waits for them, and re-layouts  4.74 us (9%)
  between operations  0.66 us (1%)
    pallas_call x1, Pallas kernels, on_device(): pl.pallas_call(functools.partial(analysis_kernel, n), out_shape=jax.Shape...  50 us
    reshape x1, local copies, waits for them, and re-layouts, on_device(): return out.reshape(sample_collection.shape)  2.52 us
    unnamed x1, local copies, waits for them, and re-layouts  2.22 us

profile of v4, /device:TPU:11, one launch (start us, length us, event | category | flops | bytes accessed | tf_op | source)
XLA Modules:
  0.0 55.4 jit_solution(17207210679142530101)
XLA Ops:
  0.7 2.2 %copy.11 = bf16[64,3,1,16,128]{4,0,3,1,2:T(8,128)(2,1)} copy(bf16[64,3,1,16,128]{4,3,2,1,0:T(8,128)(2,1)} %param.7) | data formatting | bytes 1572864 | tf_op args[0]
  2.9 50.0 %shard_map.73 = bf16[3,16,64,128]{3,2,1,0:T(8,128)(2,1)} custom-call(bf16[3,16,64,128]{3,2,1,0:T(8,128)(2,1)} %bitcast.14, f32[16,128]{1,0:T(8,128)} %bitcast.15, s32[1,512]{1,0:T(1,128)} %bitcast.16, f32[1,512]{1,0:T(1,128)} %bitcast.17, f32[1,512]{1,0:T(1,128)} %bitcast.18, s32[1,512]{1,0:T(1,128)} %bitcast.19, s32[1,1]{1,0:T(1,128)S(6)} %copy.12.count_ref), custom_call_target="tpu_custom_call" | custom-call | tf_op jit(solution)/shard_map/pallas_call | solution.py:367
  52.9 2.5 %copy.9 = bf16[64,3,1,16,128]{4,3,2,1,0:T(8,128)(2,1)} copy(bf16[64,3,1,16,128]{4,0,3,1,2:T(8,128)(2,1)} %bitcast.13) | data formatting | bytes 1572864 | tf_op jit(solution)/shard_map/reshape | solution.py:393
